TPU v7x, 32 devices: a whole 2x2x4 slice. The times are simulated.
32 devices in a mesh: parts: 2 (over y), row: 4 (over z), frame: 4 (over x, core).
Axes of the slice: x: 2, y: 2, z: 4, core: 2. Of those that a mesh axis runs over, the one named last changes fastest.
Arguments:
- latent: bfloat16 [8, 8, 16, 512], P(('parts', 'frame'), 'row'), parts along dimension 0, may hold values from -15 to 15
- qkv_weight: bfloat16 [3, 512, 512], P(None, 'frame'), may hold values from -0.125 to 0.125
- out_weight: bfloat16 [512, 512], P('frame'), may hold values from -0.25 to 0.25
- attn_gain: float32 [512], replicated, may hold values from 0.1 to 1.9
- in_weight: bfloat16 [512, 2, 2048], P(None, None, 'frame'), may hold values from -0.25 to 0.25
- depth_weight: float32 [3, 3, 2, 2048], replicated, may hold values from -2 to 2
- down_weight: bfloat16 [2048, 512], P('frame'), may hold values from -0.125 to 0.125
- mlp_gain: float32 [512], replicated, may hold values from 0.1 to 1.9
- conv_first: bfloat16 [3, 3, 3, 512, 512], P(None, None, None, 'frame'), may hold values from -0.0546875 to 0.0546875
- conv_second: bfloat16 [3, 3, 3, 512, 512], P(None, None, None, 'frame'), may hold values from -0.0546875 to 0.0546875
Outputs:
- decoded: bfloat16 [8, 8, 16, 512], P('parts', 'row', 'frame'), parts along dimension 0
There are 2 independent parts, one for each index of `parts`. A program takes and returns all parts, laid end to end along the dimension named above; an argument that names none is the same for every part. Nothing has to cross between parts.
All inputs are finite; a program needn't handle non-finite values.
Results may differ from a plain program's by a relative error of at most 0.015.
Values may be sent and summed in bfloat16 or wider, within the bound.
A program may use at most 128 MiB of HBM per device.

v0:
```python
import jax
import jax.numpy as jnp
from jax import lax
from jax.sharding import PartitionSpec as P

HEAD = 32


def padded_2(cells, sides, width):
    for axis, dim in sides:
        count = lax.axis_size(axis)
        ends = count - 1
        head = lax.slice_in_dim(cells, 0, width, axis=dim)
        tail = lax.slice_in_dim(cells, cells.shape[dim] - width, cells.shape[dim], axis=dim)
        cells = jnp.concatenate(
            [
                lax.ppermute(tail, axis, [(i, (i + 1) % count) for i in range(ends)]),
                cells,
                lax.ppermute(head, axis, [((i + 1) % count, i) for i in range(ends)]),
            ],
            axis=dim,
        )
    return cells


def norm_rows(values, gain):
    return values * lax.rsqrt(jnp.mean(values * values, axis=-1, keepdims=True) + 1e-05) * gain


def attend(packed):
    frames, height, columns = (packed.shape[0], packed.shape[1], packed.shape[2])
    width = packed.shape[4]
    heads = width // HEAD
    flat = packed.reshape(frames, height * columns, 3, heads, HEAD)
    query = jnp.maximum(flat[:, :, 0], 0)
    keys = jnp.maximum(flat[:, :, 1], 0)
    values = flat[:, :, 2]
    state = jnp.einsum("fnhd,fnhe->fhde", keys, values, preferred_element_type=jnp.float32)
    key_total = jnp.sum(keys.astype(jnp.float32), axis=1)
    state, key_total = (
        lax.psum(state.astype(jnp.bfloat16), "row").astype(jnp.float32),
        lax.psum(key_total.astype(jnp.bfloat16), "row").astype(jnp.float32),
    )
    count = height * lax.axis_size("row") * columns
    state = state / count
    key_mean = key_total / count
    query_wide = query.astype(jnp.float32)
    numer = jnp.einsum("fnhd,fhde->fnhe", query_wide, state, precision=lax.Precision.HIGHEST)
    denom = jnp.maximum(
        jnp.einsum("fnhd,fhd->fnh", query_wide, key_mean, precision=lax.Precision.HIGHEST), 1.0
    )
    return (numer / denom[..., None]).astype(jnp.bfloat16).reshape(frames, height, columns, width)


def depth_mix(inner, depth_local):
    height, columns = (inner.shape[1], inner.shape[2])
    extended = padded_2(inner, (("row", 1),), 1)
    padded = jnp.pad(extended, ((0, 0), (0, 0), (1, 1), (0, 0), (0, 0)))
    spread = jnp.zeros(inner.shape, jnp.float32)
    for shift_row in range(3):
        for shift_col in range(3):
            spread = (
                spread
                + padded[:, shift_row : shift_row + height, shift_col : shift_col + columns].astype(
                    jnp.float32
                )
                * depth_local[shift_row, shift_col]
            )
    return (spread[..., 0, :] * jax.nn.silu(spread[..., 1, :])).astype(jnp.bfloat16)


def conv_tile(extended, kernel):
    frames, padded_rows, columns, width = extended.shape
    height = padded_rows - 2
    out_width = kernel.shape[3]
    padded = jnp.pad(extended, ((1, 1), (0, 0), (1, 1), (0, 0)))
    result = jnp.zeros((frames * height * columns, out_width), jnp.float32)
    for shift_time in range(3):
        for shift_row in range(3):
            slab = padded[shift_time : shift_time + frames, shift_row : shift_row + height]
            stacked = jnp.stack(
                [slab[:, :, shift_col : shift_col + columns] for shift_col in range(3)], axis=3
            )
            result = result + jnp.einsum(
                "nci,coi->no",
                stacked.reshape(-1, 3, width),
                kernel[shift_time, shift_row],
                preferred_element_type=jnp.float32,
            )
    return result.reshape(frames, height, columns, out_width)


def local(
    latent,
    qkv_weight,
    out_weight,
    attn_gain,
    in_weight,
    depth_weight,
    down_weight,
    mlp_gain,
    conv_first,
    conv_second,
):
    frames, height, columns, width = latent.shape
    place = lax.axis_index("frame")
    packed = jnp.einsum(
        "frwc,kjc->frwkj",
        latent,
        lax.all_gather(qkv_weight, "frame", axis=1, tiled=True),
        preferred_element_type=jnp.float32,
    ).astype(jnp.bfloat16)
    mixed = attend(packed)
    section = mixed
    attn_out = jnp.einsum(
        "frwj,jc->frwc",
        section,
        lax.all_gather(out_weight, "frame", axis=0, tiled=True),
        preferred_element_type=jnp.float32,
    )
    first = (latent.astype(jnp.float32) + norm_rows(attn_out, attn_gain)).astype(jnp.bfloat16)
    inner = jax.nn.silu(
        jnp.einsum(
            "frwc,ckj->frwkj",
            first,
            lax.all_gather(in_weight, "frame", axis=2, tiled=True),
            preferred_element_type=jnp.float32,
        )
    ).astype(jnp.bfloat16)
    gated = depth_mix(inner, depth_weight)
    section = gated
    mlp_out = jnp.einsum(
        "frwj,jc->frwc",
        section,
        lax.all_gather(down_weight, "frame", axis=0, tiled=True),
        preferred_element_type=jnp.float32,
    )
    second = (first.astype(jnp.float32) + norm_rows(mlp_out, mlp_gain)).astype(jnp.bfloat16)
    gathered = lax.all_gather(second, "frame", axis=0, tiled=True)
    out_share = conv_first.shape[3]
    extended = padded_2(gathered, (("row", 1),), 2)
    activated = jax.nn.silu(conv_tile(extended, conv_first))
    global_row = lax.axis_index("row") * height - 1 + lax.iota(jnp.int32, height + 2)
    inside = ((global_row >= 0) & (global_row < height * lax.axis_size("row"))).astype(jnp.float32)
    hidden_conv = (activated * inside[None, :, None, None]).astype(jnp.bfloat16)
    joined = lax.all_gather(hidden_conv, "frame", axis=3, tiled=True)
    result = conv_tile(joined, conv_second)
    own_part = lax.dynamic_slice_in_dim(gathered, place * out_share, out_share, 3)
    final = (own_part.astype(jnp.float32) + result).astype(jnp.bfloat16)
    return lax.all_to_all(final, "frame", split_axis=2, concat_axis=3, tiled=True)


def solution(mesh):
    in_specs = (
        P(("parts", "frame"), "row", None, None),
        P(None, "frame", None),
        P("frame", None),
        P(),
        P(None, None, "frame"),
        P(),
        P("frame", None),
        P(),
        P(None, None, None, "frame", None),
        P(None, None, None, "frame", None),
    )
    out_specs = P("parts", "row", "frame", None)
    return jax.shard_map(local, mesh=mesh, in_specs=in_specs, out_specs=out_specs, check_vma=False)
```

profile of v0, /device:TPU:0, one launch (start us, length us, event | category | flops | bytes accessed | tf_op | source)
XLA Modules:
  0.0 137.9 jit_solution(649510478248561732)
XLA Ops:
  6.5 0.7 all-gather.4.cloned.1.call-update
  7.3 2.4 %copy.34 = bf16[512,2,512]{2,0,1:T(8,128)(2,1)} copy(bf16[512,2,512]{2,1,0:T(2,128)(2,1)} %param.14) | data formatting | bytes 2097152 | tf_op args[4]
  9.8 0.7 all-gather.8.cloned.1.call-update
  10.5 8.6 %all_gather.19 = bf16[512,512]{1,0:T(8,128)(2,1)S(1)} all-gather(bf16[128,512]{1,0:T(8,128)(2,1)S(1)} %copy-done.1), channel_id=1, replica_groups=mesh['parts'=2,'row'=4,'frame'=4] {'frame'}, dimensions={0}, use_global_device_ids=true | all-gather | bytes 655360 | tf_op jit(solution)/shard_map/all_gather | solution.py:118
  19.1 12.1 %all-gather.4.cloned.1.call-done = bf16[3,512,512]{2,1,0:T(8,128)(2,1)} async-done(((bf16[3,128,512]{2,1,0:T(8,128)(2,1)}), bf16[3,512,512]{2,1,0:T(8,128)(2,1)}) %all-gather.4.cloned.1.call-update) | async-done | bytes 1572880 | tf_op jit(solution)/shard_map/all_gather | solution.py:110
  31.3 2.0 %fusion.7 = bf16[2,16,3,512]{3,1,2,0:T(8,128)(2,1)S(1)} fusion(bf16[3,512,512]{2,1,0:T(8,128)(2,1)} %all-gather.4.cloned.1.call-done, bf16[1,2,16,512]{3,2,1,0:T(8,128)(2,1)S(1)} %copy-done.2), kind=kOutput, calls=%fused_computation.59 | convolution fusion | flops 50380800 | bytes 1703936 | tf_op jit(solution)/shard_map/frwc,kjc->frwkj/dot_general | solution.py:107
  34.0 21.4 %all-reduce.3 = (bf16[1,16,32,32]{3,2,1,0:T(8,128)(2,1)S(1)}, bf16[1,16,32]{2,1,0:T(8,128)(2,1)S(1)}) all-reduce(bf16[1,16,32,32]{3,2,1,0:T(8,128)(2,1)S(1)} %fusion.10, bf16[1,16,32]{2,1,0:T(8,128)(2,1)S(1)} %bitcast.373), channel_id=1, replica_groups=mesh['parts'=2,'row'=4,'frame'=4] {'row'}, use_global_device_ids=true, to_apply=%region_0.0 | all-reduce | flops 16896 | bytes 67584 | tf_op jit(solution)/shard_map/psum | solution.py:41
  55.8 0.4 fusion.28
  57.0 10.4 %all-gather.6.cloned.1.call-done = bf16[512,2,2048]{2,0,1:T(8,128)(2,1)} async-done(((bf16[512,2,512]{2,0,1:T(8,128)(2,1)}), bf16[512,2,2048]{2,0,1:T(8,128)(2,1)}) %all-gather.6.cloned.1.call-update) | async-done | bytes 4194320 | tf_op jit(solution)/shard_map/all_gather | solution.py:126
  67.3 3.0 %multiply_convert_fusion = bf16[2,16,2,2048]{3,1,2,0:T(8,128)(2,1)S(1)} fusion(bf16[512,2,2048]{2,0,1:T(8,128)(2,1)} %all-gather.6.cloned.1.call-done, bf16[1,2,16,512]{3,2,1,0:T(8,128)(2,1)S(1)} %fusion.184), kind=kOutput, calls=%fused_computation.154 | convolution fusion | flops 134873088 | bytes 4489216 | tf_op jit(solution)/shard_map/frwc,ckj->frwkj/dot_general | solution.py:123
  70.4 3.4 %collective-permute-start = (bf16[1,1,16,2,2048]{4,2,3,1,0:T(8,128)(2,1)S(1)}, bf16[1,1,16,2,2048]{4,2,3,1,0:T(8,128)(2,1)S(1)}, u32[]{:S(2)}, u32[]{:S(2)}) collective-permute-start(bf16[1,1,16,2,2048]{4,2,3,1,0:T(8,128)(2,1)S(1)} %get-tuple-element.62), channel_id=1, source_target_pairs={{0,4},{4,8},{8,12},{1,5},{5,9},{9,13},{2,6},{6,10},{10,14},{3,7},{... | collective-permute-start | bytes 393224 | tf_op jit(solution)/shard_map/ppermute | solution.py:17
  73.8 1.3 collective-permute-start.1
  75.1 1.8 %collective-permute-done = bf16[1,1,16,2,2048]{4,2,3,1,0:T(8,128)(2,1)S(1)} collective-permute-done((bf16[1,1,16,2,2048]{4,2,3,1,0:T(8,128)(2,1)S(1)}, bf16[1,1,16,2,2048]{4,2,3,1,0:T(8,128)(2,1)S(1)}, u32[]{:S(2)}, u32[]{:S(2)}) %collective-permute-start) | collective-permute-done | bytes 131104 | tf_op jit(solution)/shard_map/ppermute | solution.py:17
  76.9 4.1 %collective-permute-done.1 = bf16[1,1,16,2,2048]{4,2,3,1,0:T(8,128)(2,1)S(1)} collective-permute-done((bf16[1,1,16,2,2048]{4,2,3,1,0:T(8,128)(2,1)S(1)}, bf16[1,1,16,2,2048]{4,2,3,1,0:T(8,128)(2,1)S(1)}, u32[]{:S(2)}, u32[]{:S(2)}) %collective-permute-start.1) | collective-permute-done | bytes 131104 | tf_op jit(solution)/shard_map/ppermute | solution.py:19
  81.3 0.5 fusion.82
  81.8 9.7 %all-gather.8.cloned.1.call-done = bf16[2048,512]{1,0:T(8,128)(2,1)} async-done(((bf16[512,512]{1,0:T(8,128)(2,1)}), bf16[2048,512]{1,0:T(8,128)(2,1)}) %all-gather.8.cloned.1.call-update) | async-done | bytes 2097168 | tf_op jit(solution)/shard_map/all_gather | solution.py:135
  91.5 2.1 %multiply_reduce_fusion = (f32[2,16]{1,0:T(2,128)S(1)}, f32[2,16,512]{2,1,0:T(8,128)S(1)}) fusion(bf16[2048,512]{1,0:T(8,128)(2,1)} %all-gather.8.cloned.1.call-done, f32[1,2,16,2,2048]{4,2,3,1,0:T(8,128)S(1)} %fusion.82), kind=kOutput, calls=%fused_computation.264 | convolution fusion | flops 67534816 | bytes 2687104 | tf_op jit(solution)/shard_map/frwj,jc->frwc/dot_general | solution.py:132
  93.7 5.4 %all_gather.22 = bf16[4,2,16,512]{3,2,1,0:T(8,128)(2,1)S(1)} all-gather(bf16[1,2,16,512]{3,2,1,0:T(8,128)(2,1)S(1)} %fusion.183), channel_id=1, replica_groups=mesh['parts'=2,'row'=4,'frame'=4] {'frame'}, dimensions={0}, use_global_device_ids=true | all-gather | bytes 163840 | tf_op jit(solution)/shard_map/all_gather | solution.py:139
  99.1 3.4 %collective-permute-start.2 = (bf16[4,2,16,512]{3,2,1,0:T(8,128)(2,1)S(1)}, bf16[4,2,16,512]{3,2,1,0:T(8,128)(2,1)S(1)}, u32[]{:S(2)}, u32[]{:S(2)}) collective-permute-start(bf16[4,2,16,512]{3,2,1,0:T(8,128)(2,1)S(1)} %all_gather.22), channel_id=1, source_target_pairs={{0,4},{4,8},{8,12},{1,5},{5,9},{9,13},{2,6},{6,10},{10,14},{3,7},{... | collective-permute-start | bytes 393224 | tf_op jit(solution)/shard_map/ppermute | solution.py:17
  102.5 1.3 collective-permute-start.3
  103.8 1.9 %collective-permute-done.2 = bf16[4,2,16,512]{3,2,1,0:T(8,128)(2,1)S(1)} collective-permute-done((bf16[4,2,16,512]{3,2,1,0:T(8,128)(2,1)S(1)}, bf16[4,2,16,512]{3,2,1,0:T(8,128)(2,1)S(1)}, u32[]{:S(2)}, u32[]{:S(2)}) %collective-permute-start.2) | collective-permute-done | bytes 131104 | tf_op jit(solution)/shard_map/ppermute | solution.py:17
  105.8 4.1 %collective-permute-done.3 = bf16[4,2,16,512]{3,2,1,0:T(8,128)(2,1)S(1)} collective-permute-done((bf16[4,2,16,512]{3,2,1,0:T(8,128)(2,1)S(1)}, bf16[4,2,16,512]{3,2,1,0:T(8,128)(2,1)S(1)}, u32[]{:S(2)}, u32[]{:S(2)}) %collective-permute-start.3) | collective-permute-done | bytes 131104 | tf_op jit(solution)/shard_map/ppermute | solution.py:19
  109.9 0.8 pad_slice_fusion.23
  110.9 1.0 copy-done.5
  112.7 0.4 convolution_bitcast_fusion.6
  113.4 0.4 convolution_bitcast_fusion.4
  113.8 0.4 convolution_bitcast_fusion.3
  114.2 0.4 convolution_bitcast_fusion.2
  114.9 0.4 fusion.18
  115.4 5.9 %all_gather.23 = bf16[4,4,16,512]{3,2,1,0:T(8,128)(2,1)S(1)} all-gather(bf16[4,4,16,128]{3,2,1,0:T(8,128)(2,1)S(1)} %multiply_convert_fusion.1), channel_id=1, replica_groups=mesh['parts'=2,'row'=4,'frame'=4] {'frame'}, dimensions={3}, use_global_device_ids=true | all-gather | bytes 327680 | tf_op jit(solution)/shard_map/all_gather | solution.py:146
  124.4 6.3 %all_to_all.18 = bf16[4,2,16,128]{3,1,0,2:T(2,128)(2,1)S(1)} all-to-all(bf16[4,2,16,128]{3,1,0,2:T(2,128)(2,1)S(1)} %copy.36), channel_id=1, replica_groups=mesh['parts'=2,'row'=4,'frame'=4] {'frame'}, dimensions={2} | all-to-all | bytes 65536 | tf_op jit(solution)/shard_map/all_to_all | solution.py:150
  130.7 0.6 all_to_all.16
  (62 shorter events, 7.1 us)
Async XLA Ops:
  6.5 4.0 %copy-start.1 = (bf16[128,512]{1,0:T(8,128)(2,1)S(1)}, bf16[128,512]{1,0:T(8,128)(2,1)}, u32[]{:S(2)}) copy-start(bf16[128,512]{1,0:T(8,128)(2,1)} %param.12) | copy-start | bytes 393220
  6.5 24.7 %copy-start.2 = (bf16[1,2,16,512]{3,2,1,0:T(8,128)(2,1)S(1)}, bf16[1,2,16,512]{3,2,1,0:T(8,128)(2,1)}, u32[]{:S(2)}) copy-start(bf16[1,2,16,512]{3,2,1,0:T(8,128)(2,1)} %param.10) | copy-start | bytes 98308
  6.5 24.7 %all-gather.4.cloned.1.call-start = ((), (), s32[]{:S(2)}) async-start(), calls=%async_computation.1 | async-start | bytes 1966080 | tf_op jit(solution)/shard_map/all_gather | solution.py:110
  7.3 60.1 %all-gather.6.cloned.1.call-start = ((), (), s32[]{:S(2)}) async-start(), calls=%async_computation.2 | async-start | bytes 5242880 | tf_op jit(solution)/shard_map/all_gather | solution.py:126
  9.7 81.7 %all-gather.8.cloned.1.call-start = ((), (), s32[]{:S(2)}) async-start(), calls=%async_computation.3 | async-start | bytes 2621440 | tf_op jit(solution)/shard_map/all_gather | solution.py:135
  19.1 37.7 %copy-start.3 = (f32[512]{0:T(512)S(1)}, f32[512]{0:T(512)}, u32[]{:S(2)}) copy-start(f32[512]{0:T(512)} %param.13) | copy-start | bytes 6148
  56.9 18.2 %copy-start = (f32[3,3,2,2048]{3,2,1,0:T(2,128)S(1)}, f32[3,3,2,2048]{3,2,1,0:T(2,128)}, u32[]{:S(2)}) copy-start(f32[3,3,2,2048]{3,2,1,0:T(2,128)} %param.15) | copy-start | bytes 442372
  70.4 6.5 %collective-permute-start = (bf16[1,1,16,2,2048]{4,2,3,1,0:T(8,128)(2,1)S(1)}, bf16[1,1,16,2,2048]{4,2,3,1,0:T(8,128)(2,1)S(1)}, u32[]{:S(2)}, u32[]{:S(2)}) collective-permute-start(bf16[1,1,16,2,2048]{4,2,3,1,0:T(8,128)(2,1)S(1)} %get-tuple-element.62), channel_id=1, source_target_pairs={{0,4},{4,8},{8,12},{1,5},{5,9},{9,13},{2,6},{6,10},{10,14},{3,7},{... | collective-permute-start | bytes 393224 | tf_op jit(solution)/shard_map/ppermute | solution.py:17
  73.8 7.3 %collective-permute-start.1 = (bf16[1,1,16,2,2048]{4,2,3,1,0:T(8,128)(2,1)S(1)}, bf16[1,1,16,2,2048]{4,2,3,1,0:T(8,128)(2,1)S(1)}, u32[]{:S(2)}, u32[]{:S(2)}) collective-permute-start(bf16[1,1,16,2,2048]{4,2,3,1,0:T(8,128)(2,1)S(1)} %get-tuple-element.63), channel_id=1, source_target_pairs={{4,0},{8,4},{12,8},{5,1},{9,5},{13,9},{6,2},{10,6},{14,10},{7,3},{... | collective-permute-start | bytes 393224 | tf_op jit(solution)/shard_map/ppermute | solution.py:19
  75.1 18.4 %copy-start.4 = (f32[512]{0:T(512)S(1)}, f32[512]{0:T(512)}, u32[]{:S(2)}) copy-start(f32[512]{0:T(512)} %param.17) | copy-start | bytes 6148
  99.1 6.6 %collective-permute-start.2 = (bf16[4,2,16,512]{3,2,1,0:T(8,128)(2,1)S(1)}, bf16[4,2,16,512]{3,2,1,0:T(8,128)(2,1)S(1)}, u32[]{:S(2)}, u32[]{:S(2)}) collective-permute-start(bf16[4,2,16,512]{3,2,1,0:T(8,128)(2,1)S(1)} %all_gather.22), channel_id=1, source_target_pairs={{0,4},{4,8},{8,12},{1,5},{5,9},{9,13},{2,6},{6,10},{10,14},{3,7},{... | collective-permute-start | bytes 393224 | tf_op jit(solution)/shard_map/ppermute | solution.py:17
  102.5 7.4 %collective-permute-start.3 = (bf16[4,2,16,512]{3,2,1,0:T(8,128)(2,1)S(1)}, bf16[4,2,16,512]{3,2,1,0:T(8,128)(2,1)S(1)}, u32[]{:S(2)}, u32[]{:S(2)}) collective-permute-start(bf16[4,2,16,512]{3,2,1,0:T(8,128)(2,1)S(1)} %all_gather.22), channel_id=1, source_target_pairs={{4,0},{8,4},{12,8},{5,1},{9,5},{13,9},{6,2},{10,6},{14,10},{7,3},{... | collective-permute-start | bytes 393224 | tf_op jit(solution)/shard_map/ppermute | solution.py:19
  109.9 2.0 %copy-start.5 = (bf16[3,3,3,128,512]{4,3,2,1,0:T(8,128)(2,1)S(1)}, bf16[3,3,3,128,512]{4,3,2,1,0:T(8,128)(2,1)}, u32[]{:S(2)}) copy-start(bf16[3,3,3,128,512]{4,3,2,1,0:T(8,128)(2,1)} %param.18) | copy-start | bytes 10616836
  114.9 6.9 %copy-start.6 = (bf16[3,3,3,128,512]{4,3,2,1,0:T(8,128)(2,1)S(1)}, bf16[3,3,3,128,512]{4,3,2,1,0:T(8,128)(2,1)}, u32[]{:S(2)}) copy-start(bf16[3,3,3,128,512]{4,3,2,1,0:T(8,128)(2,1)} %param.19) | copy-start | bytes 10616836
Sparse Core Ops, SparseCore 0:
  8.9 22.3 all-gather.3
  32.8 34.4 all-gather.5
  68.9 22.5 all-gather.7
where the time goes:
time: 138 us
  blocking collectives  47.7 us (35%)
  waiting for transfers between devices  45.5 us (33%)
  matrix products  13.8 us (10%)
  between operations  13.6 us (10%)
  starting transfers between devices  9.45 us (7%)
  local copies, waits for them, and re-layouts  6.56 us (5%)
    psum x1, blocking collectives, attend(): lax.psum(state.astype(jnp.bfloat16), 'row').astype(jnp.float32)  21.4 us
    all_gather x1, waiting for transfers between devices, local(): lax.all_gather(qkv_weight, 'frame', axis=1, tiled=True)  12.1 us
    all_gather x1, waiting for transfers between devices, local(): lax.all_gather(in_weight, 'frame', axis=2, tiled=True)  10.4 us
    all_gather x1, waiting for transfers between devices, local(): lax.all_gather(down_weight, 'frame', axis=0, tiled=True)  9.69 us
    all_gather x1, blocking collectives, local(): lax.all_gather(out_weight, 'frame', axis=0, tiled=True)  8.65 us
    ppermute x2, waiting for transfers between devices, padded_2(): lax.ppermute(head, axis, [((i + 1) % count, i) for i in range(ends)])  8.23 us
    ppermute x2, starting transfers between devices, padded_2(): lax.ppermute(tail, axis, [(i, (i + 1) % count) for i in range(ends)])  6.78 us
    all_to_all x1, blocking collectives, local(): lax.all_to_all(final, 'frame', split_axis=2, concat_axis=3, tiled=True)  6.3 us
  transfers between devices with their start and end apart: 7, of which 7 were waited for; matrix products, arithmetic and copies ran while one was open for 8% of the time, Pallas kernels for 0%

commit v1 on v0

v1 whole, which is shorter than its diff:
```python
import functools

import jax
import jax.numpy as jnp
from jax import lax
from jax.experimental import pallas as pl
from jax.experimental.pallas import tpu as pltpu
from jax.sharding import PartitionSpec as P

HEAD = 32
F32 = jnp.float32
BF16 = jnp.bfloat16
MESH = pl.DeviceIdType.MESH


def dot(a, b):
    return jnp.dot(a, b, preferred_element_type=F32)


def dot_nt(a, b):
    return lax.dot_general(a, b, (((1,), (1,)), ((), ())), preferred_element_type=F32)


def dot_tn(a, b):
    return lax.dot_general(a, b, (((0,), (0,)), ((), ())), preferred_element_type=F32)


def split(values):
    high = values.astype(BF16)
    return high, (values - high.astype(F32)).astype(BF16)


def norm_rows(values, gain):
    return values * lax.rsqrt(jnp.mean(values * values, axis=-1, keepdims=True) + 1e-05) * gain


def column_shifts(flat, columns):
    count = flat.shape[0]
    at = lax.rem(lax.broadcasted_iota(jnp.int32, flat.shape, 0), columns)
    left = jnp.where(at == 0, 0.0, pltpu.roll(flat, 1, 0))
    right = jnp.where(at == columns - 1, 0.0, pltpu.roll(flat, count - 1, 0))
    return left, flat, right


def kernel(
    F,
    R,
    latent_ref,
    qkv_ref,
    out_w_ref,
    attn_gain_ref,
    in_w_hbm,
    depth_ref,
    down_hbm,
    mlp_gain_ref,
    first_hbm,
    second_hbm,
    out_ref,
    x_buf,
    ow_buf,
    st_buf,
    mx_buf,
    fi_buf,
    part_buf,
    rs_send,
    rs_buf,
    own_buf,
    s_buf,
    sh_buf,
    h_buf,
    hs_buf,
    fs_buf,
    fr_buf,
    in_w,
    down_w,
    first_w,
    second_w,
    load_sem,
    x_ssem,
    x_rsem,
    ow_ssem,
    ow_rsem,
    st_ssem,
    st_rsem,
    mx_ssem,
    mx_rsem,
    rs_ssem,
    rs_rsem,
    s_ssem,
    s_rsem,
    h_ssem,
    h_rsem,
    f_ssem,
    f_rsem,
):
    me_f = lax.axis_index("frame")
    me_r = lax.axis_index("row")
    fl, h, W, C = latent_ref.shape
    T = fl * F
    hc = qkv_ref.shape[1]
    N = in_w.shape[2]
    oc = first_w.shape[3]
    heads = hc // HEAD
    wc = W // F

    loads = [
        pltpu.make_async_copy(src, dst, load_sem.at[i])
        for i, (src, dst) in enumerate(
            ((in_w_hbm, in_w), (down_hbm, down_w), (first_hbm, first_w), (second_hbm, second_w))
        )
    ]
    for load in loads:
        load.start()

    def ahead(d):
        return lax.rem(me_f + d, F)

    def behind(d):
        return lax.rem(me_f + (F - d), F)

    def remote(src, dst, ssem, rsem, row, frame):
        return pltpu.make_async_remote_copy(
            src_ref=src,
            dst_ref=dst,
            send_sem=ssem,
            recv_sem=rsem,
            device_id={"row": row, "frame": frame},
            device_id_type=MESH,
        )

    barrier = pltpu.get_barrier_semaphore()

    def greet(row, frame):
        pl.semaphore_signal(barrier, inc=1, device_id={"row": row, "frame": frame}, device_id_type=MESH)

    for d in range(1, F):
        greet(me_r, ahead(d))
    for d in range(1, R):
        greet(lax.rem(me_r + d, R), me_f)

    @pl.when(me_r < R - 1)
    def _():
        for d in range(1, F):
            greet(me_r + 1, ahead(d))

    @pl.when(me_r > 0)
    def _():
        for d in range(1, F):
            greet(me_r - 1, ahead(d))

    neighbours = lax.div(me_r + (R - 1), R) + lax.div(2 * R - 2 - me_r, R)
    pl.semaphore_wait(barrier, F - 1 + R - 1 + (F - 1) * neighbours)

    def frames_of(index):
        return pl.ds(index * fl, fl)

    def band_start(src, buf, g, ssem, rsem):
        mine = frames_of(me_f)

        @pl.when(me_r < R - 1)
        def _():
            for d in range(F):
                remote(
                    src.at[:, h - g : h], buf.at[mine, 0:g], ssem.at[F + d], rsem.at[F + d], me_r + 1, ahead(d)
                ).start()

        @pl.when(me_r > 0)
        def _():
            for d in range(F):
                remote(
                    src.at[:, 0:g], buf.at[mine, g + h : h + 2 * g], ssem.at[2 * F + d], rsem.at[2 * F + d],
                    me_r - 1, ahead(d),
                ).start()

        for d in range(1, F):
            remote(src, buf.at[mine, g : g + h], ssem.at[d], rsem.at[d], me_r, ahead(d)).start()

    def band_wait(src, buf, g, ssem, rsem):
        for d in range(1, F):
            remote(src, buf.at[frames_of(behind(d)), g : g + h], ssem.at[d], rsem.at[d], me_r, ahead(d)).wait()

        @pl.when(me_r > 0)
        def _():
            for d in range(F):
                theirs = frames_of(behind(d))
                remote(
                    src.at[:, 0:g], buf.at[theirs, 0:g], ssem.at[2 * F + d], rsem.at[F + d], me_r - 1, ahead(d)
                ).wait()

        @pl.when(me_r < R - 1)
        def _():
            for d in range(F):
                theirs = frames_of(behind(d))
                remote(
                    src.at[:, h - g : h], buf.at[theirs, g + h : h + 2 * g], ssem.at[F + d], rsem.at[2 * F + d],
                    me_r + 1, ahead(d),
                ).wait()

    def zero_edges(buf, g):
        @pl.when(me_r == 0)
        def _():
            buf[:, 0:g] = jnp.zeros((T, g, W, C), BF16)

        @pl.when(me_r == R - 1)
        def _():
            buf[:, g + h : h + 2 * g] = jnp.zeros((T, g, W, C), BF16)

    def share_start(buf, ssem, rsem, src=None):
        for d in range(1, F):
            remote(
                buf.at[me_f] if src is None else src, buf.at[me_f], ssem.at[d], rsem.at[d], me_r, ahead(d)
            ).start()

    def share_wait(buf, ssem, rsem, src=None):
        for d in range(1, F):
            remote(
                buf.at[me_f] if src is None else src, buf.at[behind(d)], ssem.at[d], rsem.at[d], me_r, ahead(d)
            ).wait()

    band_start(latent_ref, x_buf, 1, x_ssem, x_rsem)
    x_buf[frames_of(me_f), 1 : 1 + h] = latent_ref[...]
    zero_edges(x_buf, 1)
    zero_edges(s_buf, 2)
    ow_buf[me_f] = out_w_ref[...]
    for shift in range(3):
        for t in (0, T + 1):
            sh_buf[shift, t] = jnp.zeros(sh_buf.shape[2:], BF16)
            hs_buf[shift, t] = jnp.zeros(hs_buf.shape[2:], BF16)
    band_wait(latent_ref, x_buf, 1, x_ssem, x_rsem)
    share_start(ow_buf, ow_ssem, ow_rsem, out_w_ref)

    own_x = x_buf[:, 1 : 1 + h].reshape(T * h * W, C)
    keys = jnp.maximum(dot_nt(own_x, qkv_ref[1]), 0.0).astype(BF16)
    values = dot_nt(own_x, qkv_ref[2]).astype(BF16)
    head_row = lax.div(lax.broadcasted_iota(jnp.int32, (hc, hc), 0), HEAD)
    head_col = lax.div(lax.broadcasted_iota(jnp.int32, (hc, hc), 1), HEAD)
    same_head = head_row == head_col
    n = h * W
    for t in range(T):
        outer = dot_tn(keys[t * n : (t + 1) * n], values[t * n : (t + 1) * n])
        outer = jnp.where(same_head, outer, 0.0)
        packed = outer[0:HEAD]
        for i in range(1, heads):
            packed = packed + outer[i * HEAD : (i + 1) * HEAD]
        st_buf[me_r, t * HEAD : (t + 1) * HEAD] = packed.astype(BF16)
    sums = st_buf.shape[1] - T * HEAD
    of_frame = lax.div(lax.broadcasted_iota(jnp.int32, (sums, T * n), 1), n)
    pick = jnp.where(of_frame == lax.broadcasted_iota(jnp.int32, (sums, T * n), 0), 1.0, 0.0).astype(BF16)
    st_buf[me_r, T * HEAD :] = dot(pick, keys).astype(BF16)
    for d in range(1, R):
        remote(
            st_buf.at[me_r], st_buf.at[me_r], st_ssem.at[d], st_rsem.at[d], lax.rem(me_r + d, R), me_f
        ).start()
    query = jnp.maximum(dot_nt(x_buf[...].reshape(T * (h + 2) * W, C), qkv_ref[0]), 0.0).astype(BF16)
    for d in range(1, R):
        remote(
            st_buf.at[me_r], st_buf.at[lax.rem(me_r + (R - d), R)], st_ssem.at[d], st_rsem.at[d],
            lax.rem(me_r + d, R), me_f,
        ).wait()
    total = st_buf[0].astype(F32)
    for r in range(1, R):
        total = total + st_buf[r].astype(F32)
    total = total * (1.0 / (h * R * W))

    ones = jnp.where(same_head, 1.0, 0.0).astype(BF16)
    m = (h + 2) * W
    for t in range(T):
        q = query[t * m : (t + 1) * m]
        packed = total[t * HEAD : (t + 1) * HEAD]
        state = jnp.where(same_head, jnp.concatenate([packed] * heads, axis=0), 0.0)
        high, low = split(state)
        numer = dot(q, high) + dot(q, low)
        high, low = split(q.astype(F32) * total[T * HEAD + t : T * HEAD + t + 1])
        denom = jnp.maximum(dot(high, ones) + dot(low, ones), 1.0)
        mx_buf[me_f, t * m : (t + 1) * m] = (numer / denom).astype(BF16)
    share_start(mx_buf, mx_ssem, mx_rsem)
    share_wait(ow_buf, ow_ssem, ow_rsem, out_w_ref)
    share_wait(mx_buf, mx_ssem, mx_rsem)

    attn_out = dot(mx_buf[0], ow_buf[0])
    for f in range(1, F):
        attn_out = attn_out + dot(mx_buf[f], ow_buf[f])
    latent = x_buf[...].reshape(T * m, C).astype(F32)
    first = (latent + norm_rows(attn_out, attn_gain_ref[...])).astype(BF16)
    fi_buf[...] = first.reshape(T, h + 2, W, C)

    loads[0].wait()
    spread = []
    lanes = pl.ds(pl.multiple_of(me_f * N, N), N)
    for k in range(2):
        inner = jax.nn.silu(dot(first, in_w[k])).astype(BF16).astype(F32)
        mix = jnp.zeros((T, h, W, N), F32)
        for j, moved in enumerate(column_shifts(inner, W)):
            moved = moved.reshape(T, h + 2, W, N)
            for i in range(3):
                tap = depth_ref[i, j, k : k + 1, lanes]
                mix = mix + moved[:, i : i + h] * tap.reshape(1, 1, 1, N)
        spread.append(mix)
    gated = (spread[0] * jax.nn.silu(spread[1])).astype(BF16).reshape(T * n, N)
    loads[1].wait()
    part = dot(gated, down_w[...]).reshape(T, h, W, C)
    part_buf[...] = part
    rs_send[...] = part.astype(BF16)
    for d in range(1, F):
        remote(
            rs_send.at[frames_of(ahead(d))], rs_buf.at[d], rs_ssem.at[d], rs_rsem.at[d], me_r, ahead(d)
        ).start()
    for d in range(1, F):
        remote(
            rs_send.at[frames_of(ahead(d))], rs_buf.at[d], rs_ssem.at[d], rs_rsem.at[d], me_r, ahead(d)
        ).wait()
    mlp_out = part_buf[frames_of(me_f)]
    for d in range(1, F):
        mlp_out = mlp_out + rs_buf[d].astype(F32)
    second = (
        fi_buf[frames_of(me_f), 1 : 1 + h].astype(F32)
        + norm_rows(mlp_out, mlp_gain_ref[...].reshape(1, 1, 1, C))
    ).astype(BF16)
    own_buf[...] = second
    band_start(own_buf, s_buf, 2, s_ssem, s_rsem)
    s_buf[frames_of(me_f), 2 : 2 + h] = second
    band_wait(own_buf, s_buf, 2, s_ssem, s_rsem)

    rows = h + 4
    for j, moved in enumerate(column_shifts(s_buf[...].reshape(T * rows * W, C).astype(F32), W)):
        sh_buf[j, 1 : T + 1] = moved.astype(BF16).reshape(T, rows, W, C)
    loads[2].wait()

    def conv(buf, weights, out_rows):
        acc = jnp.zeros((T * out_rows * W, oc), F32)
        for a in range(3):
            for b in range(3):
                for c in range(3):
                    slab = buf[c, a : a + T, b : b + out_rows].reshape(T * out_rows * W, C)
                    acc = acc + dot_nt(slab, weights[a, b, c])
        return acc

    active = jax.nn.silu(conv(sh_buf, first_w, h + 2))
    row = lax.rem(lax.div(lax.broadcasted_iota(jnp.int32, active.shape, 0), W), h + 2) + (me_r * h - 1)
    hidden = jnp.where((row >= 0) & (row < h * R), active, 0.0)
    h_buf[me_f] = hidden.astype(BF16)
    share_start(h_buf, h_ssem, h_rsem)
    loads[3].wait()
    share_wait(h_buf, h_ssem, h_rsem)
    for f in range(F):
        for j, moved in enumerate(column_shifts(h_buf[f].astype(F32), W)):
            hs_buf[j, 1 : T + 1, :, :, f * oc : (f + 1) * oc] = moved.astype(BF16).reshape(T, h + 2, W, oc)
    result = conv(hs_buf, second_w, h)
    for f in range(F):
        kept = s_buf[:, 2 : 2 + h, :, f * oc : (f + 1) * oc].astype(F32).reshape(T * n, oc)
        result = result + jnp.where(me_f == f, kept, 0.0)
    result = result.reshape(T, h, W, oc)
    for j in range(F):
        fs_buf[j] = result[:, :, j * wc : (j + 1) * wc]
    for d in range(1, F):
        remote(fs_buf.at[ahead(d)], fr_buf.at[me_f], f_ssem.at[d], f_rsem.at[d], me_r, ahead(d)).start()
    fr_buf[me_f] = fs_buf[me_f]
    for d in range(1, F):
        remote(fs_buf.at[ahead(d)], fr_buf.at[behind(d)], f_ssem.at[d], f_rsem.at[d], me_r, ahead(d)).wait()
    for f in range(F):
        out_ref[:, :, :, f * oc : (f + 1) * oc] = fr_buf[f].astype(BF16)


def solution(mesh):
    F, R = mesh.shape["frame"], mesh.shape["row"]

    def local(
        latent, qkv_weight, out_weight, attn_gain, in_weight, depth_weight, down_weight, mlp_gain, conv_first,
        conv_second,
    ):
        fl, h, W, C = latent.shape
        T = fl * F
        hc = qkv_weight.shape[1]
        N = in_weight.shape[2]
        oc = conv_first.shape[3]
        sums = -(-T // 16) * 16
        vmem = pl.BlockSpec(memory_space=pltpu.VMEM)
        hbm = pl.BlockSpec(memory_space=pl.ANY)
        dma = lambda count: pltpu.SemaphoreType.DMA((count,))
        return pl.pallas_call(
            functools.partial(kernel, F, R),
            out_shape=jax.ShapeDtypeStruct((T, h, W // F, C), BF16),
            in_specs=[vmem, vmem, vmem, vmem, hbm, vmem, hbm, vmem, hbm, hbm],
            out_specs=vmem,
            scratch_shapes=[
                pltpu.VMEM((T, h + 2, W, C), BF16),
                pltpu.VMEM((F, hc, C), BF16),
                pltpu.VMEM((R, T * HEAD + sums, hc), BF16),
                pltpu.VMEM((F, T * (h + 2) * W, hc), BF16),
                pltpu.VMEM((T, h + 2, W, C), BF16),
                pltpu.VMEM((T, h, W, C), F32),
                pltpu.VMEM((T, h, W, C), BF16),
                pltpu.VMEM((F, fl, h, W, C), BF16),
                pltpu.VMEM((fl, h, W, C), BF16),
                pltpu.VMEM((T, h + 4, W, C), BF16),
                pltpu.VMEM((3, T + 2, h + 4, W, C), BF16),
                pltpu.VMEM((F, T * (h + 2) * W, oc), BF16),
                pltpu.VMEM((3, T + 2, h + 2, W, C), BF16),
                pltpu.VMEM((F, T, h, W // F, oc), F32),
                pltpu.VMEM((F, T, h, W // F, oc), F32),
                pltpu.VMEM((2, C, N), BF16),
                pltpu.VMEM(down_weight.shape, BF16),
                pltpu.VMEM(conv_first.shape, BF16),
                pltpu.VMEM(conv_second.shape, BF16),
                dma(4),
                dma(3 * F), dma(3 * F),
                dma(F), dma(F),
                dma(R), dma(R),
                dma(F), dma(F),
                dma(F), dma(F),
                dma(3 * F), dma(3 * F),
                dma(F), dma(F),
                dma(F), dma(F),
            ],
            compiler_params=pltpu.CompilerParams(collective_id=0, has_side_effects=True),
        )(
            latent, qkv_weight, out_weight, attn_gain.reshape(1, C), jnp.transpose(in_weight, (1, 0, 2)),
            depth_weight, down_weight, mlp_gain.reshape(1, C), conv_first, conv_second,
        )

    in_specs = (
        P(("parts", "frame"), "row", None, None),
        P(None, "frame", None),
        P("frame", None),
        P(),
        P(None, None, "frame"),
        P(),
        P("frame", None),
        P(),
        P(None, None, None, "frame", None),
        P(None, None, None, "frame", None),
    )
    out_specs = P("parts", "row", "frame", None)
    return jax.shard_map(local, mesh=mesh, in_specs=in_specs, out_specs=out_specs, check_vma=False)
```

time: 138 us -> 48.7 us (0.35)
  blocking collectives: 47.7 us -> 0 us
  waiting for transfers between devices: 45.5 us -> 0 us
  Pallas kernels: 0 us -> 44.7 us
  matrix products: 13.8 us -> 0 us
  between operations: 13.6 us -> 0.01 us
  starting transfers between devices: 9.45 us -> 0 us
  local copies, waits for them, and re-layouts: 6.56 us -> 3.76 us
    pallas_call x0 -> x1, Pallas kernels: none -> 44.7 us  [local(): pl.pallas_call(functools.partial(kernel, F, R), out_shape=jax.ShapeDtypeS...]
    all_gather x3 -> x0, waiting for transfers between devices: 32.2 us -> none  [the longest x1 12.1 us: local(): lax.all_gather(qkv_weight, 'frame', axis=1, tiled=True)]
    psum x1 -> x0, blocking collectives: 21.4 us -> none  [attend(): lax.psum(state.astype(jnp.bfloat16), 'row').astype(jnp.float32)]
    all_gather x3 -> x0, blocking collectives: 20 us -> none  [the longest x1 8.65 us: local(): lax.all_gather(out_weight, 'frame', axis=0, tiled=True)]
    dot_general x25 -> x0, matrix products: 13.8 us -> none  [the longest x18 5.73 us: conv_tile(): jnp.einsum('nci,coi->no', stacked.reshape(-1, 3, width), kernel[shift_tim...]
    ppermute x4 -> x0, waiting for transfers between devices: 11.9 us -> none  [the longest x2 8.23 us: padded_2(): lax.ppermute(head, axis, [((i + 1) % count, i) for i in range(ends)])]
    ppermute x4 -> x0, starting transfers between devices: 9.37 us -> none  [the longest x2 6.78 us: padded_2(): lax.ppermute(tail, axis, [(i, (i + 1) % count) for i in range(ends)])]
    all_to_all x1 -> x0, blocking collectives: 6.3 us -> none  [local(): lax.all_to_all(final, 'frame', split_axis=2, concat_axis=3, tiled=True)]
  transfers between devices with their start and end apart: 7 -> 0, of which waited for: 7 -> 0; matrix products, arithmetic and copies ran while one was open for 8% -> 0% of each run, Pallas kernels for 0% -> 0%
where the time goes in v1:
time: 48.7 us; the launch traced here: 48.5 us
  Pallas kernels  44.7 us (92%)
  local copies, waits for them, and re-layouts  3.76 us (8%)
    pallas_call x1, Pallas kernels, local(): pl.pallas_call(functools.partial(kernel, F, R), out_shape=jax.ShapeDtypeS...  44.7 us
    unnamed x2, local copies, waits for them, and re-layouts  3.76 us

profile of v1, /device:TPU:0, one launch (start us, length us, event | category | flops | bytes accessed | tf_op | source)
XLA Modules:
  0.0 48.5 jit_solution(17180351292724126631)
XLA Ops:
  0.0 2.4 %copy.13 = bf16[512,2,512]{2,0,1:T(8,128)(2,1)} copy(bf16[512,2,512]{2,1,0:T(2,128)(2,1)} %param.14) | data formatting | bytes 2097152 | tf_op args[4]
  2.4 44.7 %shard_map.100 = bf16[4,2,4,512]{3,2,1,0:T(4,128)(2,1)} custom-call(bf16[1,2,16,512]{3,2,1,0:T(8,128)(2,1)} %latent_ref.1, bf16[3,128,512]{2,1,0:T(8,128)(2,1)} %qkv_ref.1, bf16[128,512]{1,0:T(8,128)(2,1)} %out_w_ref.1, f32[1,512]{1,0:T(1,128)} %bitcast.6, bf16[2,512,512]{2,1,0:T(8,128)(2,1)} %bitcast.5, f32[3,3,2,2048]{3,2,1,0:T(2,128)} %depth_ref.1, ...), custom_call_target="tpu_custom_call" | custom-call | tf_op jit(solution)/shard_map/pallas_call | solution.py:380
  47.1 1.4 %copy.15 = bf16[4,2,4,512]{3,2,1,0:T(4,128)(2,1)} copy(bf16[4,2,4,512]{3,2,1,0:T(4,128)(2,1)} %shard_map.100) | data formatting | bytes 65536

commit v2 on v1

--- a/solution.py
+++ b/solution.py
@@ -71,6 +71,7 @@
     hs_buf,
     fs_buf,
     fr_buf,
+    in_raw,
     in_w,
     down_w,
     first_w,
@@ -106,17 +107,22 @@
     loads = [
         pltpu.make_async_copy(src, dst, load_sem.at[i])
         for i, (src, dst) in enumerate(
-            ((in_w_hbm, in_w), (down_hbm, down_w), (first_hbm, first_w), (second_hbm, second_w))
+            ((in_w_hbm, in_raw), (down_hbm, down_w), (first_hbm, first_w), (second_hbm, second_w))
         )
     ]
     for load in loads:
         load.start()
 
+    chip, core, chips = lax.div(me_f, 2), lax.rem(me_f, 2), F // 2
+
+    def chip_behind(e):
+        return lax.rem(chip + (chips - e), chips)
+
     def ahead(d):
-        return lax.rem(me_f + d, F)
+        return 2 * lax.rem(chip + d // 2, chips) + lax.rem(core + d, 2)
 
     def behind(d):
-        return lax.rem(me_f + (F - d), F)
+        return 2 * chip_behind(d // 2) + lax.rem(core + d, 2)
 
     def remote(src, dst, ssem, rsem, row, frame):
         return pltpu.make_async_remote_copy(
@@ -156,29 +162,28 @@
 
     def band_start(src, buf, g, ssem, rsem):
         mine = frames_of(me_f)
+        for d in reversed(range(1, F)):
+            remote(src, buf.at[mine, g : g + h], ssem.at[d], rsem.at[d], me_r, ahead(d)).start()
 
         @pl.when(me_r < R - 1)
         def _():
-            for d in range(F):
+            for d in reversed(range(F)):
                 remote(
                     src.at[:, h - g : h], buf.at[mine, 0:g], ssem.at[F + d], rsem.at[F + d], me_r + 1, ahead(d)
                 ).start()
 
         @pl.when(me_r > 0)
         def _():
-            for d in range(F):
+            for d in reversed(range(F)):
                 remote(
                     src.at[:, 0:g], buf.at[mine, g + h : h + 2 * g], ssem.at[2 * F + d], rsem.at[2 * F + d],
                     me_r - 1, ahead(d),
                 ).start()
 
-        for d in range(1, F):
-            remote(src, buf.at[mine, g : g + h], ssem.at[d], rsem.at[d], me_r, ahead(d)).start()
-
-    def band_wait(src, buf, g, ssem, rsem):
-        for d in range(1, F):
-            remote(src, buf.at[frames_of(behind(d)), g : g + h], ssem.at[d], rsem.at[d], me_r, ahead(d)).wait()
-
+    def band_wait_own(src, buf, g, ssem, rsem, d):
+        remote(src, buf.at[frames_of(behind(d)), g : g + h], ssem.at[d], rsem.at[d], me_r, ahead(d)).wait()
+
+    def band_wait_edges(src, buf, g, ssem, rsem):
         @pl.when(me_r > 0)
         def _():
             for d in range(F):
@@ -206,13 +211,13 @@
             buf[:, g + h : h + 2 * g] = jnp.zeros((T, g, W, C), BF16)
 
     def share_start(buf, ssem, rsem, src=None):
-        for d in range(1, F):
+        for d in reversed(range(1, F)):
             remote(
                 buf.at[me_f] if src is None else src, buf.at[me_f], ssem.at[d], rsem.at[d], me_r, ahead(d)
             ).start()
 
-    def share_wait(buf, ssem, rsem, src=None):
-        for d in range(1, F):
+    def share_wait(buf, ssem, rsem, src=None, peers=range(1, F)):
+        for d in peers:
             remote(
                 buf.at[me_f] if src is None else src, buf.at[behind(d)], ssem.at[d], rsem.at[d], me_r, ahead(d)
             ).wait()
@@ -225,9 +230,9 @@
     for shift in range(3):
         for t in (0, T + 1):
             sh_buf[shift, t] = jnp.zeros(sh_buf.shape[2:], BF16)
-            hs_buf[shift, t] = jnp.zeros(hs_buf.shape[2:], BF16)
-    band_wait(latent_ref, x_buf, 1, x_ssem, x_rsem)
-    share_start(ow_buf, ow_ssem, ow_rsem, out_w_ref)
+            hs_buf[:, shift, t] = jnp.zeros((chips, *hs_buf.shape[3:]), BF16)
+    for d in range(1, F):
+        band_wait_own(latent_ref, x_buf, 1, x_ssem, x_rsem, d)
 
     own_x = x_buf[:, 1 : 1 + h].reshape(T * h * W, C)
     keys = jnp.maximum(dot_nt(own_x, qkv_ref[1]), 0.0).astype(BF16)
@@ -251,7 +256,12 @@
         remote(
             st_buf.at[me_r], st_buf.at[me_r], st_ssem.at[d], st_rsem.at[d], lax.rem(me_r + d, R), me_f
         ).start()
+    share_start(ow_buf, ow_ssem, ow_rsem, out_w_ref)
+    band_wait_edges(latent_ref, x_buf, 1, x_ssem, x_rsem)
     query = jnp.maximum(dot_nt(x_buf[...].reshape(T * (h + 2) * W, C), qkv_ref[0]), 0.0).astype(BF16)
+    loads[0].wait()
+    for k in range(2):
+        in_w[k] = in_raw[:, k, :]
     for d in range(1, R):
         remote(
             st_buf.at[me_r], st_buf.at[lax.rem(me_r + (R - d), R)], st_ssem.at[d], st_rsem.at[d],
@@ -284,7 +294,6 @@
     first = (latent + norm_rows(attn_out, attn_gain_ref[...])).astype(BF16)
     fi_buf[...] = first.reshape(T, h + 2, W, C)
 
-    loads[0].wait()
     spread = []
     lanes = pl.ds(pl.multiple_of(me_f * N, N), N)
     for k in range(2):
@@ -319,46 +328,63 @@
     own_buf[...] = second
     band_start(own_buf, s_buf, 2, s_ssem, s_rsem)
     s_buf[frames_of(me_f), 2 : 2 + h] = second
-    band_wait(own_buf, s_buf, 2, s_ssem, s_rsem)
-
-    rows = h + 4
-    for j, moved in enumerate(column_shifts(s_buf[...].reshape(T * rows * W, C).astype(F32), W)):
-        sh_buf[j, 1 : T + 1] = moved.astype(BF16).reshape(T, rows, W, C)
+
+    def place(frames, at, count, start, rows):
+        flat = s_buf[frames, start : start + rows].reshape(count * rows * W, C).astype(F32)
+        for j, moved in enumerate(column_shifts(flat, W)):
+            sh_buf[j, at, start : start + rows] = moved.astype(BF16).reshape(count, rows, W, C)
+
+    def place_own(f):
+        place(frames_of(f), pl.ds(1 + f * fl, fl), fl, 2, h)
+
+    place_own(me_f)
+    for d in range(1, F):
+        band_wait_own(own_buf, s_buf, 2, s_ssem, s_rsem, d)
+        place_own(behind(d))
+    band_wait_edges(own_buf, s_buf, 2, s_ssem, s_rsem)
+    for start in (0, h + 2):
+        place(slice(0, T), slice(1, T + 1), T, start, 2)
     loads[2].wait()
 
-    def conv(buf, weights, out_rows):
-        acc = jnp.zeros((T * out_rows * W, oc), F32)
+    def conv(acc, buf, weight, out_rows):
         for a in range(3):
             for b in range(3):
                 for c in range(3):
-                    slab = buf[c, a : a + T, b : b + out_rows].reshape(T * out_rows * W, C)
-                    acc = acc + dot_nt(slab, weights[a, b, c])
+                    slab = buf[c, a : a + T, b : b + out_rows].reshape(T * out_rows * W, buf.shape[-1])
+                    acc = acc + dot_nt(slab, weight(a, b, c))
         return acc
 
-    active = jax.nn.silu(conv(sh_buf, first_w, h + 2))
+    active = jax.nn.silu(
+        conv(jnp.zeros((T * (h + 2) * W, oc), F32), sh_buf, lambda a, b, c: first_w[a, b, c], h + 2)
+    )
     row = lax.rem(lax.div(lax.broadcasted_iota(jnp.int32, active.shape, 0), W), h + 2) + (me_r * h - 1)
     hidden = jnp.where((row >= 0) & (row < h * R), active, 0.0)
     h_buf[me_f] = hidden.astype(BF16)
     share_start(h_buf, h_ssem, h_rsem)
     loads[3].wait()
-    share_wait(h_buf, h_ssem, h_rsem)
-    for f in range(F):
-        for j, moved in enumerate(column_shifts(h_buf[f].astype(F32), W)):
-            hs_buf[j, 1 : T + 1, :, :, f * oc : (f + 1) * oc] = moved.astype(BF16).reshape(T, h + 2, W, oc)
-    result = conv(hs_buf, second_w, h)
+
+    result = jnp.zeros((T * n, oc), F32)
+    for e in range(chips):
+        share_wait(h_buf, h_ssem, h_rsem, peers=range(max(2 * e, 1), 2 * e + 2))
+        source = chip_behind(e)
+        for i in range(2):
+            for j, moved in enumerate(column_shifts(h_buf[2 * source + i].astype(F32), W)):
+                hs_buf[e, j, 1 : T + 1, :, :, i * oc : (i + 1) * oc] = moved.astype(BF16).reshape(T, h + 2, W, oc)
+        taken = pl.ds(pl.multiple_of(source * 2 * oc, 2 * oc), 2 * oc)
+        result = conv(result, hs_buf.at[e], lambda a, b, c: second_w[a, b, c, :, taken], h)
     for f in range(F):
         kept = s_buf[:, 2 : 2 + h, :, f * oc : (f + 1) * oc].astype(F32).reshape(T * n, oc)
         result = result + jnp.where(me_f == f, kept, 0.0)
     result = result.reshape(T, h, W, oc)
     for j in range(F):
-        fs_buf[j] = result[:, :, j * wc : (j + 1) * wc]
+        fs_buf[j] = result[:, :, j * wc : (j + 1) * wc].astype(BF16)
     for d in range(1, F):
         remote(fs_buf.at[ahead(d)], fr_buf.at[me_f], f_ssem.at[d], f_rsem.at[d], me_r, ahead(d)).start()
     fr_buf[me_f] = fs_buf[me_f]
     for d in range(1, F):
         remote(fs_buf.at[ahead(d)], fr_buf.at[behind(d)], f_ssem.at[d], f_rsem.at[d], me_r, ahead(d)).wait()
     for f in range(F):
-        out_ref[:, :, :, f * oc : (f + 1) * oc] = fr_buf[f].astype(BF16)
+        out_ref[:, :, :, f * oc : (f + 1) * oc] = fr_buf[f]
 
 
 def solution(mesh):
@@ -395,9 +421,10 @@
                 pltpu.VMEM((T, h + 4, W, C), BF16),
                 pltpu.VMEM((3, T + 2, h + 4, W, C), BF16),
                 pltpu.VMEM((F, T * (h + 2) * W, oc), BF16),
-                pltpu.VMEM((3, T + 2, h + 2, W, C), BF16),
-                pltpu.VMEM((F, T, h, W // F, oc), F32),
-                pltpu.VMEM((F, T, h, W // F, oc), F32),
+                pltpu.VMEM((F // 2, 3, T + 2, h + 2, W, 2 * oc), BF16),
+                pltpu.VMEM((F, T, h, W // F, oc), BF16),
+                pltpu.VMEM((F, T, h, W // F, oc), BF16),
+                pltpu.VMEM((C, 2, N), BF16),
                 pltpu.VMEM((2, C, N), BF16),
                 pltpu.VMEM(down_weight.shape, BF16),
                 pltpu.VMEM(conv_first.shape, BF16),
@@ -414,7 +441,7 @@
             ],
             compiler_params=pltpu.CompilerParams(collective_id=0, has_side_effects=True),
         )(
-            latent, qkv_weight, out_weight, attn_gain.reshape(1, C), jnp.transpose(in_weight, (1, 0, 2)),
+            latent, qkv_weight, out_weight, attn_gain.reshape(1, C), in_weight,
             depth_weight, down_weight, mlp_gain.reshape(1, C), conv_first, conv_second,
         )
 

time: 48.7 us -> 45.2 us (0.928)
  local copies, waits for them, and re-layouts: 3.76 us -> 1.39 us
  Pallas kernels: 44.7 us -> 43.6 us
    unnamed x2 -> x1, local copies, waits for them, and re-layouts: 3.76 us -> 1.39 us
    pallas_call x1, Pallas kernels: 44.7 us -> 43.6 us  [local(): pl.pallas_call(functools.partial(kernel, F, R), out_shape=jax.ShapeDtypeS...]
where the time goes in v2:
time: 45.2 us; the launch traced here: 45 us
  Pallas kernels  43.6 us (96%)
  local copies, waits for them, and re-layouts  1.39 us (3%)
    pallas_call x1, Pallas kernels, local(): pl.pallas_call(functools.partial(kernel, F, R), out_shape=jax.ShapeDtypeS...  43.6 us
    unnamed x1, local copies, waits for them, and re-layouts  1.39 us

profile of v2, /device:TPU:0, one launch (start us, length us, event | category | flops | bytes accessed | tf_op | source)
XLA Modules:
  0.0 45.0 jit_solution(13850813615581087350)
XLA Ops:
  0.0 43.6 %shard_map.100 = bf16[4,2,4,512]{3,2,1,0:T(4,128)(2,1)} custom-call(bf16[1,2,16,512]{3,2,1,0:T(8,128)(2,1)} %latent_ref.1, bf16[3,128,512]{2,1,0:T(8,128)(2,1)} %qkv_ref.1, bf16[128,512]{1,0:T(8,128)(2,1)} %out_w_ref.1, f32[1,512]{1,0:T(1,128)} %bitcast.2, bf16[512,2,512]{2,1,0:T(2,128)(2,1)} %in_w_hbm.1, f32[3,3,2,2048]{3,2,1,0:T(2,128)} %depth_ref.1, ...), custom_call_target="tpu_custom_call" | custom-call | tf_op jit(solution)/shard_map/pallas_call | solution.py:406
  43.6 1.4 %copy.12 = bf16[4,2,4,512]{3,2,1,0:T(4,128)(2,1)} copy(bf16[4,2,4,512]{3,2,1,0:T(4,128)(2,1)} %shard_map.100) | data formatting | bytes 65536

commit v3 on v2

--- a/solution.py
+++ b/solution.py
@@ -46,13 +46,13 @@
     F,
     R,
     latent_ref,
-    qkv_ref,
+    qkv_hbm,
     out_w_ref,
-    attn_gain_ref,
+    attn_gain_hbm,
     in_w_hbm,
-    depth_ref,
+    depth_hbm,
     down_hbm,
-    mlp_gain_ref,
+    mlp_gain_hbm,
     first_hbm,
     second_hbm,
     out_ref,
@@ -71,6 +71,10 @@
     hs_buf,
     fs_buf,
     fr_buf,
+    qkv_ref,
+    depth_ref,
+    attn_gain_ref,
+    mlp_gain_ref,
     in_raw,
     in_w,
     down_w,
@@ -104,15 +108,6 @@
     heads = hc // HEAD
     wc = W // F
 
-    loads = [
-        pltpu.make_async_copy(src, dst, load_sem.at[i])
-        for i, (src, dst) in enumerate(
-            ((in_w_hbm, in_raw), (down_hbm, down_w), (first_hbm, first_w), (second_hbm, second_w))
-        )
-    ]
-    for load in loads:
-        load.start()
-
     chip, core, chips = lax.div(me_f, 2), lax.rem(me_f, 2), F // 2
 
     def chip_behind(e):
@@ -134,6 +129,22 @@
             device_id_type=MESH,
         )
 
+    pairs = (
+        (in_w_hbm, in_raw),
+        (down_hbm, down_w),
+        (first_hbm, first_w),
+        (second_hbm, second_w),
+        (latent_ref, x_buf.at[pl.ds(me_f * fl, fl), 1 : 1 + h]),
+        (qkv_hbm, qkv_ref),
+        (out_w_ref, ow_buf.at[me_f]),
+        (attn_gain_hbm, attn_gain_ref),
+        (depth_hbm, depth_ref),
+        (mlp_gain_hbm, mlp_gain_ref),
+    )
+    loads = [pltpu.make_async_copy(src, dst, load_sem.at[i]) for i, (src, dst) in enumerate(pairs)]
+    loads[4].start()
+    loads[5].start()
+
     barrier = pltpu.get_barrier_semaphore()
 
     def greet(row, frame):
@@ -223,16 +234,18 @@
             ).wait()
 
     band_start(latent_ref, x_buf, 1, x_ssem, x_rsem)
-    x_buf[frames_of(me_f), 1 : 1 + h] = latent_ref[...]
+    for i in (6, 0, 7, 8, 9, 1, 2, 3):
+        loads[i].start()
     zero_edges(x_buf, 1)
     zero_edges(s_buf, 2)
-    ow_buf[me_f] = out_w_ref[...]
     for shift in range(3):
         for t in (0, T + 1):
             sh_buf[shift, t] = jnp.zeros(sh_buf.shape[2:], BF16)
             hs_buf[:, shift, t] = jnp.zeros((chips, *hs_buf.shape[3:]), BF16)
     for d in range(1, F):
         band_wait_own(latent_ref, x_buf, 1, x_ssem, x_rsem, d)
+    loads[4].wait()
+    loads[5].wait()
 
     own_x = x_buf[:, 1 : 1 + h].reshape(T * h * W, C)
     keys = jnp.maximum(dot_nt(own_x, qkv_ref[1]), 0.0).astype(BF16)
@@ -287,33 +300,42 @@
     share_wait(ow_buf, ow_ssem, ow_rsem, out_w_ref)
     share_wait(mx_buf, mx_ssem, mx_rsem)
 
-    attn_out = dot(mx_buf[0], ow_buf[0])
-    for f in range(1, F):
-        attn_out = attn_out + dot(mx_buf[f], ow_buf[f])
-    latent = x_buf[...].reshape(T * m, C).astype(F32)
-    first = (latent + norm_rows(attn_out, attn_gain_ref[...])).astype(BF16)
-    fi_buf[...] = first.reshape(T, h + 2, W, C)
-
-    spread = []
+    for i in (6, 7, 8, 9, 1):
+        loads[i].wait()
+
     lanes = pl.ds(pl.multiple_of(me_f * N, N), N)
-    for k in range(2):
-        inner = jax.nn.silu(dot(first, in_w[k])).astype(BF16).astype(F32)
-        mix = jnp.zeros((T, h, W, N), F32)
-        for j, moved in enumerate(column_shifts(inner, W)):
-            moved = moved.reshape(T, h + 2, W, N)
-            for i in range(3):
-                tap = depth_ref[i, j, k : k + 1, lanes]
-                mix = mix + moved[:, i : i + h] * tap.reshape(1, 1, 1, N)
-        spread.append(mix)
-    gated = (spread[0] * jax.nn.silu(spread[1])).astype(BF16).reshape(T * n, N)
-    loads[1].wait()
-    part = dot(gated, down_w[...]).reshape(T, h, W, C)
-    part_buf[...] = part
-    rs_send[...] = part.astype(BF16)
-    for d in range(1, F):
-        remote(
-            rs_send.at[frames_of(ahead(d))], rs_buf.at[d], rs_ssem.at[d], rs_rsem.at[d], me_r, ahead(d)
-        ).start()
+    for e in [*range(1, chips), 0]:
+        target = lax.rem(chip + e, chips)
+        count = 2 * fl
+        taken = pl.ds(target * count, count)
+        tokens = pl.ds(pl.multiple_of(target * (count * m), count * m), count * m)
+        attn_out = dot(mx_buf[0, tokens], ow_buf[0])
+        for f in range(1, F):
+            attn_out = attn_out + dot(mx_buf[f, tokens], ow_buf[f])
+        latent = x_buf[taken].reshape(count * m, C).astype(F32)
+        first = (latent + norm_rows(attn_out, attn_gain_ref[...])).astype(BF16)
+        if e == 0:
+            fi_buf[taken] = first.reshape(count, h + 2, W, C)
+
+        spread = []
+        for k in range(2):
+            inner = jax.nn.silu(dot(first, in_w[k])).astype(BF16).astype(F32)
+            mix = jnp.zeros((count, h, W, N), F32)
+            for j, moved in enumerate(column_shifts(inner, W)):
+                moved = moved.reshape(count, h + 2, W, N)
+                for i in range(3):
+                    tap = depth_ref[i, j, k : k + 1, lanes]
+                    mix = mix + moved[:, i : i + h] * tap.reshape(1, 1, 1, N)
+            spread.append(mix)
+        gated = (spread[0] * jax.nn.silu(spread[1])).astype(BF16).reshape(count * n, N)
+        part = dot(gated, down_w[...]).reshape(count, h, W, C)
+        if e == 0:
+            part_buf[taken] = part
+        rs_send[taken] = part.astype(BF16)
+        for d in range(max(2 * e, 1), 2 * e + 2):
+            remote(
+                rs_send.at[frames_of(ahead(d))], rs_buf.at[d], rs_ssem.at[d], rs_rsem.at[d], me_r, ahead(d)
+            ).start()
     for d in range(1, F):
         remote(
             rs_send.at[frames_of(ahead(d))], rs_buf.at[d], rs_ssem.at[d], rs_rsem.at[d], me_r, ahead(d)
@@ -406,7 +428,7 @@
         return pl.pallas_call(
             functools.partial(kernel, F, R),
             out_shape=jax.ShapeDtypeStruct((T, h, W // F, C), BF16),
-            in_specs=[vmem, vmem, vmem, vmem, hbm, vmem, hbm, vmem, hbm, hbm],
+            in_specs=[hbm] * 10,
             out_specs=vmem,
             scratch_shapes=[
                 pltpu.VMEM((T, h + 2, W, C), BF16),
@@ -424,12 +446,16 @@
                 pltpu.VMEM((F // 2, 3, T + 2, h + 2, W, 2 * oc), BF16),
                 pltpu.VMEM((F, T, h, W // F, oc), BF16),
                 pltpu.VMEM((F, T, h, W // F, oc), BF16),
+                pltpu.VMEM(qkv_weight.shape, BF16),
+                pltpu.VMEM(depth_weight.shape, F32),
+                pltpu.VMEM((1, C), F32),
+                pltpu.VMEM((1, C), F32),
                 pltpu.VMEM((C, 2, N), BF16),
                 pltpu.VMEM((2, C, N), BF16),
                 pltpu.VMEM(down_weight.shape, BF16),
                 pltpu.VMEM(conv_first.shape, BF16),
                 pltpu.VMEM(conv_second.shape, BF16),
-                dma(4),
+                dma(10),
                 dma(3 * F), dma(3 * F),
                 dma(F), dma(F),
                 dma(R), dma(R),

time: 45.2 us -> 43.3 us (0.958)
  Pallas kernels: 43.6 us -> 41.6 us
    pallas_call x1, Pallas kernels: 43.6 us -> 41.6 us  [local(): pl.pallas_call(functools.partial(kernel, F, R), out_shape=jax.ShapeDtypeS...]
where the time goes in v3:
time: 43.3 us; the launch traced here: 43 us
  Pallas kernels  41.6 us (96%)
  local copies, waits for them, and re-layouts  1.39 us (3%)
    pallas_call x1, Pallas kernels, local(): pl.pallas_call(functools.partial(kernel, F, R), out_shape=jax.ShapeDtypeS...  41.6 us
    unnamed x1, local copies, waits for them, and re-layouts  1.39 us

profile of v3, /device:TPU:0, one launch (start us, length us, event | category | flops | bytes accessed | tf_op | source)
XLA Modules:
  0.0 43.0 jit_solution(7381931431408936768)
XLA Ops:
  0.0 41.6 %shard_map.100 = bf16[4,2,4,512]{3,2,1,0:T(4,128)(2,1)} custom-call(bf16[1,2,16,512]{3,2,1,0:T(8,128)(2,1)} %latent_ref.1, bf16[3,128,512]{2,1,0:T(8,128)(2,1)} %qkv_hbm.1, bf16[128,512]{1,0:T(8,128)(2,1)} %out_w_ref.1, f32[1,512]{1,0:T(1,128)} %bitcast.2, bf16[512,2,512]{2,1,0:T(2,128)(2,1)} %in_w_hbm.1, f32[3,3,2,2048]{3,2,1,0:T(2,128)} %depth_hbm.1, ...), custom_call_target="tpu_custom_call" | custom-call | tf_op jit(solution)/shard_map/pallas_call | solution.py:428
  41.6 1.4 %copy.12 = bf16[4,2,4,512]{3,2,1,0:T(4,128)(2,1)} copy(bf16[4,2,4,512]{3,2,1,0:T(4,128)(2,1)} %shard_map.100) | data formatting | bytes 65536

commit v4 on v3

--- a/solution.py
+++ b/solution.py
@@ -238,10 +238,9 @@
         loads[i].start()
     zero_edges(x_buf, 1)
     zero_edges(s_buf, 2)
-    for shift in range(3):
-        for t in (0, T + 1):
-            sh_buf[shift, t] = jnp.zeros(sh_buf.shape[2:], BF16)
-            hs_buf[:, shift, t] = jnp.zeros((chips, *hs_buf.shape[3:]), BF16)
+    for t in (0, T + 1):
+        sh_buf[t] = jnp.zeros(sh_buf.shape[1:], BF16)
+        hs_buf[:, t] = jnp.zeros((chips, *hs_buf.shape[2:]), BF16)
     for d in range(1, F):
         band_wait_own(latent_ref, x_buf, 1, x_ssem, x_rsem, d)
     loads[4].wait()
@@ -351,13 +350,11 @@
     band_start(own_buf, s_buf, 2, s_ssem, s_rsem)
     s_buf[frames_of(me_f), 2 : 2 + h] = second
 
-    def place(frames, at, count, start, rows):
-        flat = s_buf[frames, start : start + rows].reshape(count * rows * W, C).astype(F32)
-        for j, moved in enumerate(column_shifts(flat, W)):
-            sh_buf[j, at, start : start + rows] = moved.astype(BF16).reshape(count, rows, W, C)
+    def place(frames, at, start, rows):
+        sh_buf[at, start : start + rows] = s_buf[frames, start : start + rows]
 
     def place_own(f):
-        place(frames_of(f), pl.ds(1 + f * fl, fl), fl, 2, h)
+        place(frames_of(f), pl.ds(1 + f * fl, fl), 2, h)
 
     place_own(me_f)
     for d in range(1, F):
@@ -365,35 +362,44 @@
         place_own(behind(d))
     band_wait_edges(own_buf, s_buf, 2, s_ssem, s_rsem)
     for start in (0, h + 2):
-        place(slice(0, T), slice(1, T + 1), T, start, 2)
+        place(slice(0, T), slice(1, T + 1), start, 2)
     loads[2].wait()
 
     def conv(acc, buf, weight, out_rows):
         for a in range(3):
             for b in range(3):
-                for c in range(3):
-                    slab = buf[c, a : a + T, b : b + out_rows].reshape(T * out_rows * W, buf.shape[-1])
-                    acc = acc + dot_nt(slab, weight(a, b, c))
+                slab = buf[a : a + T, b : b + out_rows].reshape(T * out_rows * W, buf.shape[-1])
+                acc = acc + dot_nt(slab, weight(a, b))
         return acc
 
-    active = jax.nn.silu(
-        conv(jnp.zeros((T * (h + 2) * W, oc), F32), sh_buf, lambda a, b, c: first_w[a, b, c], h + 2)
+    def join(acc):
+        return (
+            column_shifts(acc[:, 0:oc], W)[0]
+            + acc[:, oc : 2 * oc]
+            + column_shifts(acc[:, 2 * oc : 3 * oc], W)[2]
+        )
+
+    taps = conv(
+        jnp.zeros((T * (h + 2) * W, 3 * oc), F32), sh_buf, lambda a, b: first_w[a, b].reshape(3 * oc, C), h + 2
     )
+    active = jax.nn.silu(join(taps))
     row = lax.rem(lax.div(lax.broadcasted_iota(jnp.int32, active.shape, 0), W), h + 2) + (me_r * h - 1)
     hidden = jnp.where((row >= 0) & (row < h * R), active, 0.0)
     h_buf[me_f] = hidden.astype(BF16)
     share_start(h_buf, h_ssem, h_rsem)
     loads[3].wait()
 
-    result = jnp.zeros((T * n, oc), F32)
+    taps = jnp.zeros((T * n, 3 * oc), F32)
     for e in range(chips):
         share_wait(h_buf, h_ssem, h_rsem, peers=range(max(2 * e, 1), 2 * e + 2))
         source = chip_behind(e)
         for i in range(2):
-            for j, moved in enumerate(column_shifts(h_buf[2 * source + i].astype(F32), W)):
-                hs_buf[e, j, 1 : T + 1, :, :, i * oc : (i + 1) * oc] = moved.astype(BF16).reshape(T, h + 2, W, oc)
+            hs_buf[e, 1 : T + 1, :, :, i * oc : (i + 1) * oc] = h_buf[2 * source + i].reshape(T, h + 2, W, oc)
         taken = pl.ds(pl.multiple_of(source * 2 * oc, 2 * oc), 2 * oc)
-        result = conv(result, hs_buf.at[e], lambda a, b, c: second_w[a, b, c, :, taken], h)
+        taps = conv(
+            taps, hs_buf.at[e], lambda a, b: second_w[a, b, :, :, taken].reshape(3 * oc, 2 * oc), h
+        )
+    result = join(taps)
     for f in range(F):
         kept = s_buf[:, 2 : 2 + h, :, f * oc : (f + 1) * oc].astype(F32).reshape(T * n, oc)
         result = result + jnp.where(me_f == f, kept, 0.0)
@@ -441,9 +447,9 @@
                 pltpu.VMEM((F, fl, h, W, C), BF16),
                 pltpu.VMEM((fl, h, W, C), BF16),
                 pltpu.VMEM((T, h + 4, W, C), BF16),
-                pltpu.VMEM((3, T + 2, h + 4, W, C), BF16),
+                pltpu.VMEM((T + 2, h + 4, W, C), BF16),
                 pltpu.VMEM((F, T * (h + 2) * W, oc), BF16),
-                pltpu.VMEM((F // 2, 3, T + 2, h + 2, W, 2 * oc), BF16),
+                pltpu.VMEM((F // 2, T + 2, h + 2, W, 2 * oc), BF16),
                 pltpu.VMEM((F, T, h, W // F, oc), BF16),
                 pltpu.VMEM((F, T, h, W // F, oc), BF16),
                 pltpu.VMEM(qkv_weight.shape, BF16),

time: 43.3 us -> 41.4 us (0.956)
  Pallas kernels: 41.6 us -> 39.8 us
    pallas_call x1, Pallas kernels: 41.6 us -> 39.8 us  [local(): pl.pallas_call(functools.partial(kernel, F, R), out_shape=jax.ShapeDtypeS...]
where the time goes in v4:
time: 41.4 us; the launch traced here: 41.2 us
  Pallas kernels  39.8 us (96%)
  local copies, waits for them, and re-layouts  1.39 us (3%)
    pallas_call x1, Pallas kernels, local(): pl.pallas_call(functools.partial(kernel, F, R), out_shape=jax.ShapeDtypeS...  39.8 us
    unnamed x1, local copies, waits for them, and re-layouts  1.39 us

profile of v4, /device:TPU:0, one launch (start us, length us, event | category | flops | bytes accessed | tf_op | source)
XLA Modules:
  0.0 41.2 jit_solution(2919534631439498056)
XLA Ops:
  0.0 39.8 %shard_map.100 = bf16[4,2,4,512]{3,2,1,0:T(4,128)(2,1)} custom-call(bf16[1,2,16,512]{3,2,1,0:T(8,128)(2,1)} %latent_ref.1, bf16[3,128,512]{2,1,0:T(8,128)(2,1)} %qkv_hbm.1, bf16[128,512]{1,0:T(8,128)(2,1)} %out_w_ref.1, f32[1,512]{1,0:T(1,128)} %bitcast.2, bf16[512,2,512]{2,1,0:T(2,128)(2,1)} %in_w_hbm.1, f32[3,3,2,2048]{3,2,1,0:T(2,128)} %depth_hbm.1, ...), custom_call_target="tpu_custom_call" | custom-call | tf_op jit(solution)/shard_map/pallas_call | solution.py:434
  39.8 1.4 %copy.12 = bf16[4,2,4,512]{3,2,1,0:T(4,128)(2,1)} copy(bf16[4,2,4,512]{3,2,1,0:T(4,128)(2,1)} %shard_map.100) | data formatting | bytes 65536
